TPU v7x, 128 devices: a whole 4x4x4 slice. The times are simulated.
128 devices in a mesh: section: 8 (over z_hi, y), dp: 16 (over z_lo, x, core).
Axes of the slice: x: 4, y: 4, z: 4 (z_hi: 2, z_lo: 2; z = z_hi * 2 + z_lo), core: 2. Of those that a mesh axis runs over, the one named last changes fastest.
Arguments:
- queries: bfloat16 [8, 32, 128, 4096], P('section', 'dp'), may hold values from -240 to 240, as said below
- image_tokens: bfloat16 [32, 192, 8192], P('dp', 'section'), may hold values from -6 to 6
- key_weight: bfloat16 [8, 8192, 512], P('section'), may hold values from -0.0625 to 0.0625
- value_weight: bfloat16 [8, 8192, 512], P('section'), may hold values from -0.0625 to 0.0625
- cotangent: bfloat16 [8, 32, 128, 4096], P('section', 'dp'), may hold values from -6 to 6
- tile_counts: int32 [32], P('dp'), may hold values from 1 to 4
- text_lengths: int32 [32], P('dp'), may hold values from 32 to 128, as said below
Outputs:
- query_gradient: bfloat16 [8, 32, 128, 4096], P('section', 'dp')
- image_grad: bfloat16 [32, 192, 8192], P('dp', 'section')
- key_weight_grad: bfloat16 [8, 8192, 512], P('section', 'dp')
- value_weight_grad: bfloat16 [8, 8192, 512], P('section', 'dp')
Inputs may be any that keep to these rules, and one draw needn't show every extreme that they name: queries of one row share one scale. `text_lengths`: the live text tokens of a sample come first.
All inputs are finite; a program needn't handle non-finite values.
Results may differ from a plain program's by a relative error of at most 0.025.
The roundings to bfloat16 on the way count: a program that leaves them out, or rounds other values in their place, can miss the bound.
Values may be sent and summed in bfloat16 or wider, within the bound.
A program may use at most 192 MiB of HBM per device.

v0:
```python
import math
import jax
import jax.numpy as jnp
from jax import lax
from jax.sharding import PartitionSpec as P

QUERY_HEADS = 32
KEY_VALUE_HEADS = 4
HEAD_SIZE = 128
MAX_TILES = 4


def attend_one(queries, key_rows, value_rows, cotangent, key_limit, row_limit):
    total_rows = queries.shape[0]
    total_keys = key_rows.shape[0]
    group_width = QUERY_HEADS // KEY_VALUE_HEADS
    heads_of_queries = queries.reshape(total_rows, KEY_VALUE_HEADS, group_width, HEAD_SIZE)
    heads_of_keys = key_rows.reshape(total_keys, KEY_VALUE_HEADS, HEAD_SIZE)
    heads_of_values = value_rows.reshape(total_keys, KEY_VALUE_HEADS, HEAD_SIZE)
    row_live = (jnp.arange(total_rows) < row_limit)[:, None]
    active_cotangent = jnp.where(row_live, cotangent, jnp.zeros_like(cotangent))
    head_gradient = active_cotangent.reshape(total_rows, KEY_VALUE_HEADS, group_width, HEAD_SIZE)
    scaling = 1.0 / math.sqrt(HEAD_SIZE)
    scores = (
        jnp.einsum(
            "lhgd,nhd->hgln", heads_of_queries, heads_of_keys, preferred_element_type=jnp.float32
        )
        * scaling
    )
    key_live = jnp.arange(total_keys) < key_limit
    scores = jnp.where(key_live, scores, -jnp.inf)
    row_max = jnp.max(scores, axis=-1, keepdims=True)
    raised = jnp.exp(scores - row_max)
    weights = raised / jnp.sum(raised, axis=-1, keepdims=True)
    weights_low = weights.astype(jnp.bfloat16)
    value_gradient = jnp.einsum(
        "hgln,lhgd->nhd", weights_low, head_gradient, preferred_element_type=jnp.float32
    ).astype(jnp.bfloat16)
    prob_grad = jnp.einsum(
        "lhgd,nhd->hgln", head_gradient, heads_of_values, preferred_element_type=jnp.float32
    )
    row_dot = jnp.sum(weights * prob_grad, axis=-1, keepdims=True)
    score_grad = (weights * (prob_grad - row_dot) * scaling).astype(jnp.bfloat16)
    query_gradient = jnp.einsum(
        "hgln,nhd->lhgd", score_grad, heads_of_keys, preferred_element_type=jnp.float32
    ).astype(jnp.bfloat16)
    key_gradient = jnp.einsum(
        "hgln,lhgd->nhd", score_grad, heads_of_queries, preferred_element_type=jnp.float32
    ).astype(jnp.bfloat16)
    return (
        query_gradient.reshape(total_rows, QUERY_HEADS * HEAD_SIZE),
        key_gradient.reshape(total_keys, KEY_VALUE_HEADS * HEAD_SIZE),
        value_gradient.reshape(total_keys, KEY_VALUE_HEADS * HEAD_SIZE),
    )


def project(tokens, weight):
    return jnp.dot(tokens, weight, preferred_element_type=jnp.float32).astype(jnp.bfloat16)


def shards(queries, image_tokens, key_weight, value_weight, cotangent, tile_counts, text_lengths):
    gathered = lax.all_gather(image_tokens, "section", axis=1, tiled=True)
    samples_here = gathered.shape[0]
    image_len = gathered.shape[1]
    model_width = gathered.shape[2]
    tile_len = image_len // MAX_TILES
    w_key = key_weight[0]
    w_value = value_weight[0]
    query_local = queries[0]
    cotan_local = cotangent[0]
    query_list = []
    key_list = []
    value_list = []
    flat_tokens = gathered.reshape(samples_here * image_len, model_width)
    keys_all = project(flat_tokens, w_key).reshape(samples_here, image_len, -1)
    values_all = project(flat_tokens, w_value).reshape(samples_here, image_len, -1)
    for sample_index in range(samples_here):
        query_gradient, key_gradient, value_gradient = attend_one(
            query_local[sample_index],
            keys_all[sample_index],
            values_all[sample_index],
            cotan_local[sample_index],
            tile_counts[sample_index] * tile_len,
            text_lengths[sample_index],
        )
        query_list.append(query_gradient)
        key_list.append(key_gradient)
        value_list.append(value_gradient)
    query_out = jnp.stack(query_list)[None]
    key_grads = jnp.stack(key_list)
    value_grads = jnp.stack(value_list)
    image_term = jnp.einsum("stk,dk->std", key_grads, w_key, preferred_element_type=jnp.float32)
    image_term = image_term + jnp.einsum(
        "stk,dk->std", value_grads, w_value, preferred_element_type=jnp.float32
    )
    image_out = lax.psum_scatter(
        image_term.astype(jnp.bfloat16), "section", scatter_dimension=1, tiled=True
    )
    key_term = jnp.einsum("std,stk->dk", gathered, key_grads, preferred_element_type=jnp.float32)
    value_term = jnp.einsum(
        "std,stk->dk", gathered, value_grads, preferred_element_type=jnp.float32
    )
    key_sum, value_sum = (
        lax.psum_scatter(
            key_term.astype(jnp.bfloat16), "dp", scatter_dimension=0, tiled=True
        ).astype(jnp.float32),
        lax.psum_scatter(
            value_term.astype(jnp.bfloat16), "dp", scatter_dimension=0, tiled=True
        ).astype(jnp.float32),
    )
    return (
        query_out,
        image_out,
        key_sum.astype(jnp.bfloat16)[None],
        value_sum.astype(jnp.bfloat16)[None],
    )


def solution(mesh):
    placed = (
        P("section", "dp", None, None),
        P("dp", "section", None),
        P("section", None, None),
        P("section", None, None),
        P("section", "dp", None, None),
        P("dp"),
        P("dp"),
    )
    return jax.shard_map(
        shards,
        mesh=mesh,
        in_specs=placed,
        out_specs=(
            P("section", "dp", None, None),
            P("dp", "section", None),
            P("section", "dp", None),
            P("section", "dp", None),
        ),
        check_vma=False,
    )
```

profile of v0, /device:TPU:0, one launch (start us, length us, event | category | flops | bytes accessed | tf_op | source)
XLA Modules:
  0.0 456.2 jit_solution(1482975594506760739)
XLA Ops:
  18.3 84.2 %all-gather.2.cloned.1.call-done = bf16[2,192,8192]{2,1,0:T(8,128)(2,1)} async-done(((bf16[2,24,8192]{2,1,0:T(8,128)(2,1)}), bf16[2,192,8192]{2,1,0:T(8,128)(2,1)}) %all-gather.2.cloned.1.call-update) | async-done | bytes 6291472 | tf_op jit(solution)/shard_map/all_gather | solution.py:62
  102.4 8.6 %fusion.44 = bf16[384,512]{1,0:T(8,128)(2,1)S(1)} fusion(bf16[384,8192]{1,0:T(8,128)(2,1)} %bitcast.203, bf16[1,8192,512]{2,1,0:T(8,128)(2,1)} %param.10), kind=kOutput, calls=%fused_computation.56 | convolution fusion | flops 3221422080 | bytes 15073280 | tf_op jit(solution)/shard_map/dot_general | solution.py:58
  111.2 8.6 %fusion.41 = bf16[384,512]{1,0:T(8,128)(2,1)S(1)} fusion(bf16[384,8192]{1,0:T(8,128)(2,1)} %bitcast.204, bf16[1,8192,512]{2,1,0:T(8,128)(2,1)} %param.9), kind=kOutput, calls=%fused_computation.55 | convolution fusion | flops 3221422080 | bytes 15073280 | tf_op jit(solution)/shard_map/dot_general | solution.py:58
  123.9 2.3 fusion.72
  126.2 3.7 fusion.116
  129.9 3.4 fusion.68
  133.3 6.6 %fusion.63 = bf16[192,4,128]{2,0,1:T(8,128)(2,1)} fusion(bf16[128,4,8,128]{0,3,2,1:T(8,128)(2,1)S(1)} %bitcast.215, f32[4,192,128,8]{2,1,3,0:T(8,128)} %fusion.72, f32[4,8,128,192]{2,3,1,0:T(8,128)} %get-tuple-element.29, f32[4,8,128]{2,1,0:T(8,128)S(1)} %get-tuple-element.28), kind=kOutput, calls=%fused_computation.65 | convolution fusion | flops 206934208 | bytes 7553024 | tf_op jit(solution)/shard_map/hgln,lhgd->nhd/dot_general | solution.py:47
  142.3 2.4 fusion.71
  144.7 2.7 fusion.121
  147.4 2.7 fusion.65
  150.1 5.7 %fusion.64 = bf16[192,4,128]{2,0,1:T(8,128)(2,1)S(1)} fusion(bf16[128,4,8,128]{0,3,2,1:T(8,128)(2,1)S(1)} %bitcast.213, f32[4,192,128,8]{2,1,3,0:T(8,128)} %fusion.71, f32[4,8,128,192]{2,3,1,0:T(8,128)} %get-tuple-element.31, f32[4,8,128]{2,1,0:T(8,128)S(1)} %get-tuple-element.30), kind=kOutput, calls=%fused_computation.66 | convolution fusion | flops 206934208 | bytes 7553024 | tf_op jit(solution)/shard_map/hgln,lhgd->nhd/dot_general | solution.py:47
  156.6 11.8 %fusion.7 = f32[2,192,8192]{2,1,0:T(8,128)} fusion(bf16[2,192,512]{2,1,0:T(8,128)(2,1)S(1)} %constant_dynamic-update-slice_fusion, bf16[1,8192,512]{2,1,0:T(8,128)(2,1)} %param.9), kind=kOutput, calls=%fused_computation.10 | convolution fusion | flops 3221225472 | bytes 21364736 | tf_op jit(solution)/shard_map/stk,dk->std/dot_general | solution.py:92
  168.3 12.6 %add_convert_fusion = bf16[2,192,8192]{2,1,0:T(8,128)(2,1)} fusion(f32[2,192,8192]{2,1,0:T(8,128)} %fusion.7, bf16[2,192,512]{2,1,0:T(8,128)(2,1)S(1)} %constant_dynamic-update-slice_fusion.2, bf16[1,8192,512]{2,1,0:T(8,128)(2,1)} %param.10), kind=kOutput, calls=%fused_computation.6 | convolution fusion | flops 3227516928 | bytes 27656192 | tf_op jit(solution)/shard_map/stk,dk->std/dot_general | solution.py:93
  180.9 11.1 %copy.93 = bf16[2,192,8192]{2,0,1:T(2,128)(2,1)S(1)} copy(bf16[2,192,8192]{2,1,0:T(8,128)(2,1)} %add_convert_fusion) | data formatting | bytes 12582912
  192.0 6.9 %copy.99 = bf16[24,8,2,8192]{3,1,2,0:T(8,128)(2,1)} copy(bf16[24,8,2,8192]{3,2,1,0:T(2,128)(2,1)S(1)} %bitcast.206) | data formatting | bytes 12582912
  199.0 9.5 %fusion.4 = bf16[8192,512]{0,1:T(8,128)(2,1)} fusion(bf16[2,192,512]{2,1,0:T(8,128)(2,1)S(1)} %constant_dynamic-update-slice_fusion, bf16[2,192,8192]{2,1,0:T(8,128)(2,1)} %all-gather.2.cloned.1.call-done), kind=kOutput, calls=%fused_computation.7 | convolution fusion | flops 3225419776 | bytes 15073280 | tf_op jit(solution)/shard_map/std,stk->dk/dot_general | solution.py:99
  208.6 9.7 %fusion.5 = bf16[8192,512]{0,1:T(8,128)(2,1)} fusion(bf16[2,192,512]{2,1,0:T(8,128)(2,1)S(1)} %constant_dynamic-update-slice_fusion.2, bf16[2,192,8192]{2,1,0:T(8,128)(2,1)} %all-gather.2.cloned.1.call-done), kind=kOutput, calls=%fused_computation.8 | convolution fusion | flops 3225419776 | bytes 15073280 | tf_op jit(solution)/shard_map/std,stk->dk/dot_general | solution.py:100
  219.3 6.1 %convolution_convert_fusion = bf16[4,128,8,128]{3,1,2,0:T(8,128)(2,1)S(1)} fusion(f32[4,192,128,8]{2,1,3,0:T(8,128)} %fusion.72, bf16[192,4,128,1]{2,1,0,3:T(4,128)(2,1)S(1)} %bitcast.225, f32[4,8,128,192]{2,3,1,0:T(8,128)} %get-tuple-element.29, f32[4,8,128]{2,1,0:T(8,128)S(1)} %copy-done.7), kind=kOutput, calls=%fused_computation.49 | convolution fusion | flops 207360192 | bytes 7553024 | tf_op jit(solution)/shard_map/hgln,nhd->lhgd/dot_general | solution.py:44
  225.9 6.4 %convolution_convert_fusion.1 = bf16[4,128,8,128]{3,1,2,0:T(8,128)(2,1)S(1)} fusion(f32[4,192,128,8]{2,1,3,0:T(8,128)} %fusion.71, bf16[192,4,128,1]{2,1,0,3:T(4,128)(2,1)S(1)} %bitcast.223, f32[4,8,128,192]{2,3,1,0:T(8,128)} %get-tuple-element.31, f32[4,8,128]{2,1,0:T(8,128)S(1)} %get-tuple-element.30), kind=kOutput, calls=%fused_computation.50 | convolution fusion | flops 207360192 | bytes 7553024 | tf_op jit(solution)/shard_map/hgln,nhd->lhgd/dot_general | solution.py:44
  234.3 62.0 %reduce-scatter.10.cloned.1.call-done = bf16[24,16384]{1,0:T(8,128)(2,1)} async-done(((bf16[192,16384]{1,0:T(8,128)(2,1)}), bf16[24,16384]{1,0:T(8,128)(2,1)}) %reduce-scatter.10.cloned.1.call-update) | async-done | bytes 786448
  296.3 2.6 reshape.77
  300.2 71.6 %reduce-scatter.6.cloned.1.call-done = bf16[512,512]{0,1:T(8,128)(2,1)} async-done(((bf16[8192,512]{0,1:T(8,128)(2,1)}), bf16[512,512]{0,1:T(8,128)(2,1)}) %reduce-scatter.6.cloned.1.call-update) | async-done | bytes 524304 | tf_op jit(solution)/shard_map/reduce_scatter | solution.py:104
  373.9 73.7 %reduce-scatter.8.cloned.1.call-done = bf16[512,512]{0,1:T(8,128)(2,1)} async-done(((bf16[8192,512]{0,1:T(8,128)(2,1)}), bf16[512,512]{0,1:T(8,128)(2,1)}) %reduce-scatter.8.cloned.1.call-update) | async-done | bytes 524304 | tf_op jit(solution)/shard_map/reduce_scatter | solution.py:107
  447.6 2.0 copy.66
  (59 shorter events, 24.0 us)
Async XLA Ops:
  7.2 95.3 %all-gather.2.cloned.1.call-start = ((), (), s32[]{:S(2)}) async-start(), calls=%async_computation.3 | async-start | bytes 7077888 | tf_op jit(solution)/shard_map/all_gather | solution.py:62
  7.9 288.4 %reduce-scatter.10.cloned.1.call-start = ((), (), s32[]{:S(2)}) async-start(), calls=%async_computation.6 | async-start | bytes 7077888
  13.6 2.0 copy-start
  15.7 0.7 copy-start.5
  119.8 6.4 %copy-start.2 = (bf16[1,1,128,4096]{2,3,1,0:T(8,128)(2,1)S(1)}, bf16[1,1,128,4096]{2,3,1,0:T(8,128)(2,1)}, u32[]{:S(2)}) copy-start(bf16[1,1,128,4096]{2,3,1,0:T(8,128)(2,1)} %copy.96) | copy-start | bytes 3145732
  129.9 3.4 copy-start.6
  139.8 4.8 %copy-start.1 = (bf16[1,1,128,4096]{2,3,1,0:T(8,128)(2,1)S(1)}, bf16[1,1,128,4096]{2,3,1,0:T(8,128)(2,1)}, u32[]{:S(2)}) copy-start(bf16[1,1,128,4096]{2,3,1,0:T(8,128)(2,1)} %copy.95) | copy-start | bytes 3145732
  139.8 4.8 %copy-start.3 = (bf16[192,4,128]{2,1,0:T(4,128)(2,1)S(1)}, bf16[192,4,128]{2,1,0:T(4,128)(2,1)}, u32[]{:S(2)}) copy-start(bf16[192,4,128]{2,1,0:T(4,128)(2,1)} %reshape_squeeze.18) | copy-start | bytes 589828
  198.9 172.9 %reduce-scatter.6.cloned.1.call-start = ((), (), s32[]{:S(2)}) async-start(), calls=%async_computation.4 | async-start | bytes 8912896 | tf_op jit(solution)/shard_map/reduce_scatter | solution.py:104
  208.5 239.1 %reduce-scatter.8.cloned.1.call-start = ((), (), s32[]{:S(2)}) async-start(), calls=%async_computation.5 | async-start | bytes 8912896 | tf_op jit(solution)/shard_map/reduce_scatter | solution.py:107
  218.3 0.9 copy-start.4
  218.3 0.9 copy-start.7
Sparse Core Ops, SparseCore 0:
  10.3 92.1 all-gather.1
  199.0 97.2 reduce-scatter.9
  298.9 72.8 reduce-scatter.5
  374.2 73.3 reduce-scatter.7
where the time goes:
time: 457 us; the launch traced here: 456 us
  waiting for transfers between devices  292 us (64%)
  matrix products  103 us (23%)
  local copies, waits for them, and re-layouts  42.9 us (9%)
  between operations  15.3 us (3%)
    all_gather x1, waiting for transfers between devices, shards(): gathered = lax.all_gather(image_tokens, 'section', axis=1, tiled=True)  84.2 us
    reduce_scatter x1, waiting for transfers between devices, shards(): lax.psum_scatter(value_term.astype(jnp.bfloat16), 'dp', scatter_dimension...  73.7 us
    reduce_scatter x1, waiting for transfers between devices, shards(): lax.psum_scatter(key_term.astype(jnp.bfloat16), 'dp', scatter_dimension=0...  71.6 us
    unnamed x5, waiting for transfers between devices  62.7 us
    unnamed x29, local copies, waits for them, and re-layouts  30.9 us
    dot_general x2, matrix products, project(): jnp.dot(tokens, weight, preferred_element_type=jnp.float32)  17.2 us
    dot_general x1, matrix products, shards(): jnp.einsum('stk,dk->std', value_grads, w_value, preferred_element_type=jn...  12.6 us
    dot_general x2, matrix products, attend_one(): jnp.einsum('hgln,nhd->lhgd', score_grad, heads_of_keys, preferred_element...  12.5 us
  transfers between devices with their start and end apart: 4, of which 4 were waited for; matrix products, arithmetic and copies ran while one was open for 11% of the time, Pallas kernels for 0%

commit v1 on v0

--- a/solution.py
+++ b/solution.py
@@ -59,7 +59,10 @@
 
 
 def shards(queries, image_tokens, key_weight, value_weight, cotangent, tile_counts, text_lengths):
-    gathered = lax.all_gather(image_tokens, "section", axis=1, tiled=True)
+    gathered = jnp.concatenate(
+        lax.all_to_all(jnp.stack([image_tokens] * lax.axis_size("section")), "section", 0, 0),
+        axis=1,
+    )
     samples_here = gathered.shape[0]
     image_len = gathered.shape[1]
     model_width = gathered.shape[2]

time: 457 us -> 473 us (1.035)
  starting transfers between devices: 0.16 us -> 8.12 us
  local copies, waits for them, and re-layouts: 42.9 us -> 49.7 us
    all_gather x1 -> x0, waiting for transfers between devices: 84.2 us -> none  [shards(): gathered = lax.all_gather(image_tokens, 'section', axis=1, tiled=True)]
    all_to_all x0 -> x1, waiting for transfers between devices: none -> 63.8 us  [shards(): lax.all_to_all(jnp.stack([image_tokens] * lax.axis_size('section')), 'sec...]
    unnamed x5 -> x4, waiting for transfers between devices: 62.7 us -> 84.8 us
    all_to_all x0 -> x1, starting transfers between devices: none -> 8 us  [shards(): lax.all_to_all(jnp.stack([image_tokens] * lax.axis_size('section')), 'sec...]
    unnamed x29 -> x33, local copies, waits for them, and re-layouts: 30.9 us -> 31 us
  transfers between devices with their start and end apart: 4 -> 4, of which waited for: 4 -> 4; matrix products, arithmetic and copies ran while one was open for 11% -> 10% of each run, Pallas kernels for 0% -> 0%
where the time goes in v1:
time: 473 us
  waiting for transfers between devices  294 us (62%)
  matrix products  103 us (22%)
  local copies, waits for them, and re-layouts  49.7 us (11%)
  between operations  15.3 us (3%)
  starting transfers between devices  8.12 us (2%)
    unnamed x4, waiting for transfers between devices  84.8 us
    reduce_scatter x1, waiting for transfers between devices, shards(): lax.psum_scatter(value_term.astype(jnp.bfloat16), 'dp', scatter_dimension...  73.7 us
    reduce_scatter x1, waiting for transfers between devices, shards(): lax.psum_scatter(key_term.astype(jnp.bfloat16), 'dp', scatter_dimension=0...  71.6 us
    all_to_all x1, waiting for transfers between devices, shards(): lax.all_to_all(jnp.stack([image_tokens] * lax.axis_size('section')), 'sec...  63.8 us
    unnamed x33, local copies, waits for them, and re-layouts  31 us
    dot_general x2, matrix products, project(): jnp.dot(tokens, weight, preferred_element_type=jnp.float32)  16.9 us
    dot_general x1, matrix products, shards(): jnp.einsum('stk,dk->std', value_grads, w_value, preferred_element_type=jn...  12.8 us
    dot_general x2, matrix products, attend_one(): jnp.einsum('hgln,nhd->lhgd', score_grad, heads_of_keys, preferred_element...  12.4 us
  transfers between devices with their start and end apart: 4, of which 4 were waited for; matrix products, arithmetic and copies ran while one was open for 10% of the time, Pallas kernels for 0%

profile of v1, /device:TPU:0, one launch (start us, length us, event | category | flops | bytes accessed | tf_op | source)
XLA Modules:
  0.0 472.5 jit_solution(7471263317103301857)
XLA Ops:
  7.2 4.5 stack.8
  11.7 8.0 %all-to-all-start = ((bf16[8,2,24,8192]{3,2,1,0:T(8,128)(2,1)}), bf16[8,2,24,8192]{3,2,1,0:T(8,128)(2,1)}, u32[]{:S(2)}, u32[]{:S(2)}) async-start(bf16[8,2,24,8192]{3,2,1,0:T(8,128)(2,1)} %stack.8), calls=%async_computation | async-start | bytes 12582912 | tf_op jit(solution)/shard_map/all_to_all | solution.py:63
  29.4 63.8 %all-to-all-done = bf16[8,2,24,8192]{3,2,1,0:T(8,128)(2,1)} async-done(((bf16[8,2,24,8192]{3,2,1,0:T(8,128)(2,1)}), bf16[8,2,24,8192]{3,2,1,0:T(8,128)(2,1)}, u32[]{:S(2)}, u32[]{:S(2)}) %all-to-all-start) | async-done | bytes 6291488 | tf_op jit(solution)/shard_map/all_to_all | solution.py:63
  93.2 3.2 copy.68
  96.4 8.3 %fusion.44 = bf16[384,512]{1,0:T(8,128)(2,1)S(1)} fusion(bf16[384,8192]{1,0:T(8,128)(2,1)S(1)} %bitcast.207, bf16[1,8192,512]{2,1,0:T(8,128)(2,1)} %param.10), kind=kOutput, calls=%fused_computation.56 | convolution fusion | flops 3221422080 | bytes 15073280 | tf_op jit(solution)/shard_map/dot_general | solution.py:58
  104.8 8.6 %fusion.41 = bf16[384,512]{1,0:T(8,128)(2,1)S(1)} fusion(bf16[384,8192]{1,0:T(8,128)(2,1)} %bitcast.208, bf16[1,8192,512]{2,1,0:T(8,128)(2,1)} %param.9), kind=kOutput, calls=%fused_computation.55 | convolution fusion | flops 3221422080 | bytes 15073280 | tf_op jit(solution)/shard_map/dot_general | solution.py:58
  119.9 3.7 fusion.116
  123.5 3.4 fusion.68
  126.9 6.6 %fusion.63 = bf16[192,4,128]{2,0,1:T(8,128)(2,1)} fusion(bf16[128,4,8,128]{0,3,2,1:T(8,128)(2,1)S(1)} %bitcast.221, f32[4,192,128,8]{2,1,3,0:T(8,128)} %fusion.72, f32[4,8,128,192]{2,3,1,0:T(8,128)} %get-tuple-element.33, f32[4,8,128]{2,1,0:T(8,128)S(1)} %get-tuple-element.32), kind=kOutput, calls=%fused_computation.65 | convolution fusion | flops 206934208 | bytes 7553024 | tf_op jit(solution)/shard_map/hgln,lhgd->nhd/dot_general | solution.py:47
  138.3 2.7 fusion.121
  141.0 2.7 fusion.65
  143.7 5.7 %fusion.64 = bf16[192,4,128]{2,0,1:T(8,128)(2,1)S(1)} fusion(bf16[128,4,8,128]{0,3,2,1:T(8,128)(2,1)S(1)} %bitcast.219, f32[4,192,128,8]{2,1,3,0:T(8,128)} %fusion.71, f32[4,8,128,192]{2,3,1,0:T(8,128)} %get-tuple-element.35, f32[4,8,128]{2,1,0:T(8,128)S(1)} %get-tuple-element.34), kind=kOutput, calls=%fused_computation.66 | convolution fusion | flops 206934208 | bytes 7553024 | tf_op jit(solution)/shard_map/hgln,lhgd->nhd/dot_general | solution.py:47
  150.0 11.8 %fusion.7 = f32[2,192,8192]{2,1,0:T(8,128)} fusion(bf16[2,192,512]{2,1,0:T(8,128)(2,1)S(1)} %constant_dynamic-update-slice_fusion, bf16[1,8192,512]{2,1,0:T(8,128)(2,1)} %param.9), kind=kOutput, calls=%fused_computation.10 | convolution fusion | flops 3221225472 | bytes 21364736 | tf_op jit(solution)/shard_map/stk,dk->std/dot_general | solution.py:95
  161.8 12.8 %add_convert_fusion = bf16[2,192,8192]{2,1,0:T(8,128)(2,1)} fusion(f32[2,192,8192]{2,1,0:T(8,128)} %fusion.7, bf16[2,192,512]{2,1,0:T(8,128)(2,1)S(1)} %constant_dynamic-update-slice_fusion.2, bf16[1,8192,512]{2,1,0:T(8,128)(2,1)} %param.10), kind=kOutput, calls=%fused_computation.6 | convolution fusion | flops 3227516928 | bytes 27656192 | tf_op jit(solution)/shard_map/stk,dk->std/dot_general | solution.py:96
  174.6 11.1 %copy.117 = bf16[2,192,8192]{2,0,1:T(2,128)(2,1)S(1)} copy(bf16[2,192,8192]{2,1,0:T(8,128)(2,1)} %add_convert_fusion) | data formatting | bytes 12582912
  185.7 6.9 %copy.123 = bf16[24,8,2,8192]{3,1,2,0:T(8,128)(2,1)} copy(bf16[24,8,2,8192]{3,2,1,0:T(2,128)(2,1)S(1)} %bitcast.212) | data formatting | bytes 12582912
  192.7 9.5 %fusion.4 = bf16[8192,512]{0,1:T(8,128)(2,1)} fusion(bf16[2,192,512]{2,1,0:T(8,128)(2,1)S(1)} %constant_dynamic-update-slice_fusion, bf16[2,192,8192]{2,1,0:T(8,128)(2,1)} %bitcast.209), kind=kOutput, calls=%fused_computation.7 | convolution fusion | flops 3225419776 | bytes 15073280 | tf_op jit(solution)/shard_map/std,stk->dk/dot_general | solution.py:102
  202.3 9.8 %fusion.5 = bf16[8192,512]{0,1:T(8,128)(2,1)} fusion(bf16[2,192,512]{2,1,0:T(8,128)(2,1)S(1)} %constant_dynamic-update-slice_fusion.2, bf16[2,192,8192]{2,1,0:T(8,128)(2,1)} %bitcast.210), kind=kOutput, calls=%fused_computation.8 | convolution fusion | flops 3225419776 | bytes 15073280 | tf_op jit(solution)/shard_map/std,stk->dk/dot_general | solution.py:103
  213.0 6.0 %convolution_convert_fusion = bf16[4,128,8,128]{3,1,2,0:T(8,128)(2,1)S(1)} fusion(f32[4,192,128,8]{2,1,3,0:T(8,128)} %fusion.72, bf16[192,4,128,1]{2,1,0,3:T(4,128)(2,1)S(1)} %bitcast.231, f32[4,8,128,192]{2,3,1,0:T(8,128)} %get-tuple-element.33, f32[4,8,128]{2,1,0:T(8,128)S(1)} %copy-done.9), kind=kOutput, calls=%fused_computation.49 | convolution fusion | flops 207360192 | bytes 7553024 | tf_op jit(solution)/shard_map/hgln,nhd->lhgd/dot_general | solution.py:44
  219.5 6.4 %convolution_convert_fusion.1 = bf16[4,128,8,128]{3,1,2,0:T(8,128)(2,1)S(1)} fusion(f32[4,192,128,8]{2,1,3,0:T(8,128)} %fusion.71, bf16[192,4,128,1]{2,1,0,3:T(4,128)(2,1)S(1)} %bitcast.229, f32[4,8,128,192]{2,3,1,0:T(8,128)} %get-tuple-element.35, f32[4,8,128]{2,1,0:T(8,128)S(1)} %get-tuple-element.34), kind=kOutput, calls=%fused_computation.50 | convolution fusion | flops 207360192 | bytes 7553024 | tf_op jit(solution)/shard_map/hgln,nhd->lhgd/dot_general | solution.py:44
  228.0 84.8 %reduce-scatter.10.cloned.1.call-done = bf16[24,16384]{1,0:T(8,128)(2,1)} async-done(((bf16[192,16384]{1,0:T(8,128)(2,1)}), bf16[24,16384]{1,0:T(8,128)(2,1)}) %reduce-scatter.10.cloned.1.call-update) | async-done | bytes 786448
  312.7 2.6 reshape.83
  316.6 71.6 %reduce-scatter.6.cloned.1.call-done = bf16[512,512]{0,1:T(8,128)(2,1)} async-done(((bf16[8192,512]{0,1:T(8,128)(2,1)}), bf16[512,512]{0,1:T(8,128)(2,1)}) %reduce-scatter.6.cloned.1.call-update) | async-done | bytes 524304 | tf_op jit(solution)/shard_map/reduce_scatter | solution.py:107
  390.2 73.7 %reduce-scatter.8.cloned.1.call-done = bf16[512,512]{0,1:T(8,128)(2,1)} async-done(((bf16[8192,512]{0,1:T(8,128)(2,1)}), bf16[512,512]{0,1:T(8,128)(2,1)}) %reduce-scatter.8.cloned.1.call-update) | async-done | bytes 524304 | tf_op jit(solution)/shard_map/reduce_scatter | solution.py:110
  (64 shorter events, 29.2 us)
Async XLA Ops:
  11.7 8.0 %copy-start.6 = (s32[2]{0:T(128)S(1)}, s32[2]{0:T(128)}, u32[]{:S(2)}) copy-start(s32[2]{0:T(128)} %param.12) | copy-start | bytes 28
  11.7 81.5 %all-to-all-start = ((bf16[8,2,24,8192]{3,2,1,0:T(8,128)(2,1)}), bf16[8,2,24,8192]{3,2,1,0:T(8,128)(2,1)}, u32[]{:S(2)}, u32[]{:S(2)}) async-start(bf16[8,2,24,8192]{3,2,1,0:T(8,128)(2,1)} %stack.8), calls=%async_computation | async-start | bytes 12582912 | tf_op jit(solution)/shard_map/all_to_all | solution.py:63
  19.7 293.1 %reduce-scatter.10.cloned.1.call-start = ((), (), s32[]{:S(2)}) async-start(), calls=%async_computation.6 | async-start | bytes 7077888
  24.7 2.0 copy-start.1
  26.8 0.7 copy-start.7
  96.4 8.3 %copy-start = (bf16[8,2,24,8192]{3,2,0,1:T(8,128)(2,1)}, bf16[8,2,24,8192]{3,2,0,1:T(8,128)(2,1)S(1)}, u32[]{:S(2)}) copy-start(bf16[8,2,24,8192]{3,2,0,1:T(8,128)(2,1)S(1)} %copy.68) | copy-start | bytes 18874372
  113.5 6.4 %copy-start.3 = (bf16[1,1,128,4096]{2,3,1,0:T(8,128)(2,1)S(1)}, bf16[1,1,128,4096]{2,3,1,0:T(8,128)(2,1)}, u32[]{:S(2)}) copy-start(bf16[1,1,128,4096]{2,3,1,0:T(8,128)(2,1)} %copy.120) | copy-start | bytes 3145732
  123.5 3.4 copy-start.8
  133.5 4.8 %copy-start.2 = (bf16[1,1,128,4096]{2,3,1,0:T(8,128)(2,1)S(1)}, bf16[1,1,128,4096]{2,3,1,0:T(8,128)(2,1)}, u32[]{:S(2)}) copy-start(bf16[1,1,128,4096]{2,3,1,0:T(8,128)(2,1)} %copy.119) | copy-start | bytes 3145732
  133.5 4.8 %copy-start.4 = (bf16[192,4,128]{2,1,0:T(4,128)(2,1)S(1)}, bf16[192,4,128]{2,1,0:T(4,128)(2,1)}, u32[]{:S(2)}) copy-start(bf16[192,4,128]{2,1,0:T(4,128)(2,1)} %reshape_squeeze.18) | copy-start | bytes 589828
  192.6 195.6 %reduce-scatter.6.cloned.1.call-start = ((), (), s32[]{:S(2)}) async-start(), calls=%async_computation.4 | async-start | bytes 8912896 | tf_op jit(solution)/shard_map/reduce_scatter | solution.py:107
  202.2 261.7 %reduce-scatter.8.cloned.1.call-start = ((), (), s32[]{:S(2)}) async-start(), calls=%async_computation.5 | async-start | bytes 8912896 | tf_op jit(solution)/shard_map/reduce_scatter | solution.py:110
  212.1 0.9 copy-start.5
  212.1 0.9 copy-start.9
Sparse Core Ops, SparseCore 0:
  192.7 119.9 reduce-scatter.9
  315.3 72.8 reduce-scatter.5
  390.7 73.1 reduce-scatter.7
